TPU v7x, 32 devices: a whole 2x2x4 slice. The times are simulated.
32 devices in a mesh: slab: 8 (over z, x), head: 4 (over y, core).
Axes of the slice: x: 2, y: 2, z: 4, core: 2. Of those that a mesh axis runs over, the one named last changes fastest.
Arguments:
- atom_feats: bfloat16 [2, 4096, 128], P(None, 'slab'), may hold values from -16 to 16
- pair_feats: bfloat16 [4096, 16, 128], P('slab'), may hold values from -8 to 330
- tok_slot: int32 [4096], P('slab'), may hold values from 0 to 255, as said below
- w_proj: bfloat16 [4, 128, 128], P(None, None, 'head'), may hold values from -0.5 to 0.5
- w_out: bfloat16 [128, 128], P('head'), may hold values from -0.5 to 0.5
- w_pair: bfloat16 [16, 4], P(None, 'head'), may hold values from -1.2 to 1.2
- w_tok: bfloat16 [128, 768], P(None, 'head'), may hold values from -0.5 to 0.5
- d_tok: bfloat16 [2, 256, 768], P(None, 'slab', 'head'), may hold values from -6 to 6
Outputs:
- tok_act: bfloat16 [2, 256, 768], P(None, 'slab', 'head')
- grad_proj: float32 [4, 128, 128], P(None, None, 'head')
- grad_out: float32 [128, 128], P('head')
- grad_pair: float32 [16, 4], P(None, 'head')
- grad_tok: float32 [128, 768], P(None, 'head')
Inputs may be any that keep to these rules, and one draw needn't show every extreme that they name: `tok_slot`: never falling. The atoms s * 512 to (s + 1) * 512 - 1 use slots s * 32 to s * 32 + n - 1, each at least once, with n from 16 to 32; the first of these atoms is in slot s * 32. The last slab and one other use all 32 slots.
All inputs are finite; a program needn't handle non-finite values.
Results may differ from a plain program's by a relative error of at most 0.023.
Values may be sent and summed in bfloat16 or wider, within the bound.
A program may use at most 64 MiB of HBM per device.

v0:
```python
import jax
import jax.numpy as jnp
from jax import lax
from jax.sharding import PartitionSpec as P

Q_WIN = 32
K_WIN = 128
RIM = 48


EPSILON = 1e-05


def extended_2(cells, sides, width):
    for axis, dim in sides:
        count = lax.axis_size(axis)
        ends = count - 1
        head = lax.slice_in_dim(cells, 0, width, axis=dim)
        tail = lax.slice_in_dim(cells, cells.shape[dim] - width, cells.shape[dim], axis=dim)
        cells = jnp.concatenate(
            [
                lax.ppermute(tail, axis, [(i, (i + 1) % count) for i in range(ends)]),
                cells,
                lax.ppermute(head, axis, [((i + 1) % count, i) for i in range(ends)]),
            ],
            axis=dim,
        )
    return cells


def key_windows(extended, block_count):
    leading = extended.shape[:-2]
    last_width = extended.shape[-1]
    row_total = block_count * Q_WIN
    pieces = []
    for offset in range(K_WIN // Q_WIN):
        segment = lax.slice_in_dim(
            extended, Q_WIN * offset, Q_WIN * offset + row_total, axis=extended.ndim - 2
        )
        pieces.append(segment.reshape(leading + (block_count, Q_WIN, last_width)))
    return jnp.concatenate(pieces, axis=-2)


def key_unwindowed_rows(windowed, block_count):
    leading = windowed.shape[:-3]
    last_width = windowed.shape[-1]
    row_total = block_count * Q_WIN
    margin = K_WIN - Q_WIN
    summed = None
    for offset in range(K_WIN // Q_WIN):
        segment = windowed[..., Q_WIN * offset : Q_WIN * (offset + 1), :].reshape(
            leading + (row_total, last_width)
        )
        padding = [(0, 0)] * len(leading) + [(Q_WIN * offset, margin - Q_WIN * offset), (0, 0)]
        segment = jnp.pad(segment, padding)
        summed = segment if summed is None else summed + segment
    return summed


def on_device(atom_feats, pair_feats, tok_slot, w_proj, w_out, w_pair, w_tok, d_tok):
    samples, atom_count, feature_width = atom_feats.shape
    head_width = w_proj.shape[2]
    block_count = atom_count // Q_WIN
    slot_count = d_tok.shape[1]
    slab_index = lax.axis_index("slab")
    slab_total = lax.axis_size("slab")
    score_scale = head_width ** (-0.5)
    feats_float = atom_feats.astype(jnp.float32)
    centered = feats_float - jnp.mean(feats_float, axis=2, keepdims=True)
    variance = jnp.mean(centered * centered, axis=2, keepdims=True)
    normed = (centered * lax.rsqrt(variance + EPSILON)).astype(jnp.bfloat16)
    projected = jnp.einsum("saw,fwd->fsad", normed, w_proj, preferred_element_type=jnp.float32)
    queries = (projected[0] * score_scale).astype(jnp.bfloat16)
    keys_local = projected[1].astype(jnp.bfloat16)
    values_local = projected[2].astype(jnp.bfloat16)
    gating = jax.nn.sigmoid(projected[3])
    stacked = jnp.stack([keys_local, values_local])
    extended = extended_2(stacked, (("slab", 2),), RIM)
    windowed = key_windows(extended, block_count)
    key_window_rows = windowed[0]
    value_window_rows = windowed[1]
    query_block_rows = queries.reshape(samples, block_count, Q_WIN, head_width)
    pair_bias_terms = jnp.einsum(
        "acj,c->aj", pair_feats, w_pair[:, 0], preferred_element_type=jnp.float32
    )
    pair_bias_terms = pair_bias_terms.reshape(block_count, Q_WIN, K_WIN)
    positions = (
        slab_index * atom_count
        + Q_WIN * jnp.arange(block_count, dtype=jnp.int32)[:, None]
        - RIM
        + jnp.arange(K_WIN, dtype=jnp.int32)[None, :]
    )
    in_range = (positions >= 0) & (positions < atom_count * slab_total)
    attention_scores = (
        jnp.einsum(
            "sbqd,sbkd->sbqk", query_block_rows, key_window_rows, preferred_element_type=jnp.float32
        )
        + pair_bias_terms[None]
    )
    attention_scores = jnp.where(in_range[None, :, None, :], attention_scores, -jnp.inf)
    highest = jnp.max(attention_scores, axis=3, keepdims=True)
    exponent = jnp.exp(attention_scores - highest)
    attn_weights = exponent / jnp.sum(exponent, axis=3, keepdims=True)
    weight_half_precision = attn_weights.astype(jnp.bfloat16)
    attended_output = jnp.einsum(
        "sbqk,sbkd->sbqd",
        weight_half_precision,
        value_window_rows,
        preferred_element_type=jnp.float32,
    )
    attended_output = attended_output.reshape(samples, atom_count, head_width)
    heads_out = (gating * attended_output).astype(jnp.bfloat16)
    head_part = jnp.einsum(
        "nsad,ndw->nsaw",
        lax.all_gather(heads_out[None], "head", axis=0, tiled=True),
        lax.all_gather(w_out[None], "head", axis=0, tiled=True),
        preferred_element_type=jnp.float32,
    )
    rounded = lax.optimization_barrier(head_part.astype(jnp.bfloat16)).astype(jnp.float32)
    attn_sum = jnp.sum(rounded, axis=0)
    mixed_half = (feats_float + attn_sum).astype(jnp.bfloat16)
    pre_act = jnp.einsum("saw,wh->sah", mixed_half, w_tok, preferred_element_type=jnp.float32)
    act_gate = jax.nn.sigmoid(pre_act)
    atom_act = (pre_act * act_gate).astype(jnp.bfloat16)
    own_slots = slab_index * slot_count + jnp.arange(slot_count, dtype=jnp.int32)
    member = (tok_slot[:, None] == own_slots[None, :]).astype(jnp.bfloat16)
    counts = jnp.sum(member, axis=0, dtype=jnp.float32)
    divisor = jnp.maximum(counts, 1.0)
    token_sums = jnp.einsum("at,sah->sth", member, atom_act, preferred_element_type=jnp.float32)
    tok_act = (token_sums / divisor[None, :, None]).astype(jnp.bfloat16)
    tok_grad = (d_tok.astype(jnp.float32) / divisor[None, :, None]).astype(jnp.bfloat16)
    spread = jnp.einsum("at,sth->sah", member, tok_grad, preferred_element_type=jnp.float32)
    slope = act_gate * (1.0 + pre_act * (1.0 - act_gate))
    act_grad = (spread * slope).astype(jnp.bfloat16)
    grad_tok_local = jnp.einsum(
        "saw,sah->wh", mixed_half, act_grad, preferred_element_type=jnp.float32
    )
    mixed_terms = jnp.einsum("sah,wh->saw", act_grad, w_tok, preferred_element_type=jnp.float32)
    mixed_grad = lax.psum(mixed_terms.astype(jnp.bfloat16), "head")
    out_grad = jnp.einsum("saw,dw->sad", mixed_grad, w_out, preferred_element_type=jnp.float32)
    grad_out_local = jnp.einsum(
        "sad,saw->dw", heads_out, mixed_grad, preferred_element_type=jnp.float32
    )
    att_grad = (gating * out_grad).astype(jnp.bfloat16)
    gate_grad = (out_grad * attended_output * gating * (1.0 - gating)).astype(jnp.bfloat16)
    attention_block_rows = att_grad.reshape(samples, block_count, Q_WIN, head_width)
    probability_gradient = jnp.einsum(
        "sbqd,sbkd->sbqk",
        attention_block_rows,
        value_window_rows,
        preferred_element_type=jnp.float32,
    )
    score_grad = (
        attn_weights
        * (
            probability_gradient
            - jnp.sum(attn_weights * probability_gradient, axis=3, keepdims=True)
        )
    ).astype(jnp.bfloat16)
    query_gradient = score_scale * jnp.einsum(
        "sbqk,sbkd->sbqd", score_grad, key_window_rows, preferred_element_type=jnp.float32
    )
    query_gradient = query_gradient.reshape(samples, atom_count, head_width).astype(jnp.bfloat16)
    key_win_grad = jnp.einsum(
        "sbqk,sbqd->sbkd", score_grad, query_block_rows, preferred_element_type=jnp.float32
    )
    value_win_grad = jnp.einsum(
        "sbqk,sbqd->sbkd",
        weight_half_precision,
        attention_block_rows,
        preferred_element_type=jnp.float32,
    )
    spilled = key_unwindowed_rows(jnp.stack([key_win_grad, value_win_grad]), block_count)
    rim_local = jnp.concatenate([spilled[:, :, :RIM], spilled[:, :, RIM + atom_count :]], axis=2)
    returned = extended_2(rim_local.astype(jnp.bfloat16), (("slab", 2),), RIM).astype(
        rim_local.dtype
    )
    from_before = returned[:, :, :RIM]
    from_after = returned[:, :, 3 * RIM :]
    own_part = spilled[:, :, RIM : RIM + atom_count]
    own_part = own_part + jnp.pad(from_before, ((0, 0), (0, 0), (0, atom_count - RIM), (0, 0)))
    own_part = own_part + jnp.pad(from_after, ((0, 0), (0, 0), (atom_count - RIM, 0), (0, 0)))
    kv_grad = own_part.astype(jnp.bfloat16)
    grads_stack = jnp.stack([query_gradient, kv_grad[0], kv_grad[1], gate_grad])
    grad_proj_local = jnp.einsum(
        "saw,fsad->fwd", normed, grads_stack, preferred_element_type=jnp.float32
    )
    bias_grad = (
        jnp.sum(score_grad, axis=0, dtype=jnp.float32)
        .astype(jnp.bfloat16)
        .reshape(atom_count, K_WIN)
    )
    grad_pair_local = jnp.einsum(
        "acj,aj->c", pair_feats, bias_grad, preferred_element_type=jnp.float32
    )[:, None]
    factor = (samples * atom_count * slab_total) ** (-0.5)
    grad_proj_total, grad_out_total, grad_pair_total, grad_tok_total = lax.psum(
        (grad_proj_local, grad_out_local, grad_pair_local, grad_tok_local), "slab"
    )
    return (
        tok_act,
        grad_proj_total * factor,
        grad_out_total * factor,
        grad_pair_total * factor,
        grad_tok_total * factor,
    )


def solution(mesh):
    return jax.shard_map(
        on_device,
        mesh=mesh,
        in_specs=(
            P(None, "slab", None),
            P("slab", None, None),
            P("slab"),
            P(None, None, "head"),
            P("head", None),
            P(None, "head"),
            P(None, "head"),
            P(None, "slab", "head"),
        ),
        out_specs=(
            P(None, "slab", "head"),
            P(None, None, "head"),
            P("head", None),
            P(None, "head"),
            P(None, "head"),
        ),
        check_vma=False,
    )
```

profile of v0, /device:TPU:0, one launch (start us, length us, event | category | flops | bytes accessed | tf_op | source)
XLA Modules:
  0.0 244.7 jit_solution(9373553838993672769)
XLA Ops:
  7.2 1.2 convert_reduce_fusion.1
  8.5 1.3 fusion.14
  9.9 1.5 fusion.76
  11.4 4.9 %collective-permute-start = (bf16[2,2,48,32]{2,3,0,1:T(8,128)(2,1)S(1)}, bf16[2,2,48,32]{2,3,0,1:T(8,128)(2,1)S(1)}, u32[]{:S(2)}, u32[]{:S(2)}) collective-permute-start(bf16[2,2,48,32]{2,3,0,1:T(8,128)(2,1)S(1)} %get-tuple-element.19), channel_id=1, source_target_pairs={{0,4},{4,8},{8,12},{12,16},{16,20},{20,24},{24,28},{1,5},{5,9},{9,... | collective-permute-start | bytes 36872 | tf_op jit(solution)/shard_map/ppermute | solution.py:22
  16.3 1.3 collective-permute-start.1
  17.6 0.7 slice.103
  18.3 0.9 convert_reduce_fusion.2
  20.4 5.6 %all-gather = bf16[128,128]{1,0:T(8,128)(2,1)} all-gather(bf16[32,128]{1,0:T(8,128)(2,1)S(1)} %copy-done.20), channel_id=2, replica_groups=mesh['slab'=8,'head'=4] {'head'}, dimensions={0}, use_global_device_ids=true | all-gather | bytes 40960 | tf_op jit(solution)/shard_map/all_gather | solution.py:116
  26.7 1.7 fusion.37
  28.4 1.2 reshape.129
  29.7 0.9 copy.25
  30.9 0.9 copy.26
  32.1 0.9 copy.28
  33.5 2.0 pad_maximum_fusion.1
  35.8 0.8 copy-done.6
  36.6 1.0 fusion.77
  37.6 3.8 %fusion.29 = f32[2,16,32,32]{3,2,1,0:T(8,128)} fusion(bf16[2,2,16,128,32]{3,4,2,1,0:T(8,128)(2,1)S(1)} %pad_maximum_fusion.1, f32[2,16,32]{2,1,0:T(8,128)S(1)} %get-tuple-element.33, f32[2,16,32,128]{3,2,1,0:T(8,128)} %copy-done.6), kind=kOutput, calls=%fused_computation.63 | convolution fusion | flops 8782975 | bytes 1458176 | tf_op jit(solution)/shard_map/sbqk,sbkd->sbqd/dot_general | solution.py:105
  41.5 1.9 copy.48
  43.4 1.3 copy.47
  44.6 1.0 multiply_convert_fusion.3
  45.6 5.8 %all_gather.6 = bf16[4,2,512,32]{2,3,0,1:T(8,128)(2,1)S(1)} all-gather(bf16[1,2,512,32]{2,3,0,1:T(8,128)(2,1)S(1)} %multiply_convert_fusion.3), channel_id=1, replica_groups=mesh['slab'=8,'head'=4] {'head'}, dimensions={0}, use_global_device_ids=true | all-gather | bytes 327680 | tf_op jit(solution)/shard_map/all_gather | solution.py:115
  52.4 1.0 fusion.8
  54.2 1.1 convolution_convert_fusion.1
  55.5 0.9 convolution_bitcast_fusion.4
  56.4 34.3 %all-reduce.11.cloned.1.call-done = bf16[2,512,128]{2,1,0:T(8,128)(2,1)} async-done(((bf16[2,512,128]{2,1,0:T(8,128)(2,1)}), bf16[2,512,128]{2,1,0:T(8,128)(2,1)}) %all-reduce.11.cloned.1.call-update) | async-done | bytes 262160 | tf_op jit(solution)/shard_map/psum | solution.py:139
  90.7 1.9 fusion.42
  92.8 3.8 %convolution_bitcast_fusion.1 = f32[1,2,16,128,32]{3,4,2,1,0:T(8,128)} fusion(bf16[2,16,32,32]{2,1,3,0:T(8,128)(2,1)S(1)} %reshape.135, f32[2,16,32]{2,1,0:T(8,128)S(1)} %get-tuple-element.33, f32[2,16,32,128]{3,2,1,0:T(8,128)} %copy-done.6), kind=kOutput, calls=%fused_computation.14 | convolution fusion | flops 8782975 | bytes 1118208 | tf_op jit(solution)/shard_map/sbqk,sbqd->sbkd/dot_general | solution.py:167
  96.6 1.6 multiply_reduce_fusion
  98.6 1.0 fusion.6
  99.8 1.0 convolution_bitcast_fusion.7
  100.8 2.2 fusion.10
  103.0 1.6 copy.35
  104.6 2.3 reshape.136
  106.9 2.8 %copy.36 = f32[2,2,16,32,32]{3,2,4,1,0:T(8,128)} copy(f32[2,2,16,32,32]{3,4,2,1,0:T(8,128)} %get-tuple-element.14) | data formatting | bytes 524288 | tf_op jit(solution)/shard_map/slice | solution.py:51
  109.7 2.3 reshape.137
  112.1 2.8 %copy.38 = f32[2,2,16,32,32]{3,2,4,1,0:T(8,128)} copy(f32[2,2,16,32,32]{3,4,2,1,0:T(8,128)} %get-tuple-element.15) | data formatting | bytes 524288 | tf_op jit(solution)/shard_map/slice | solution.py:51
  114.9 2.3 reshape.139
  117.2 1.6 copy.37
  118.8 1.7 reshape.138
  120.4 1.5 fusion.72
  122.0 3.4 %collective-permute-start.2 = (bf16[2,2,48,32]{2,3,1,0:T(8,128)(2,1)S(1)}, bf16[2,2,48,32]{2,3,1,0:T(8,128)(2,1)S(1)}, u32[]{:S(2)}, u32[]{:S(2)}) collective-permute-start(bf16[2,2,48,32]{2,3,1,0:T(8,128)(2,1)S(1)} %get-tuple-element.21), channel_id=1, source_target_pairs={{0,4},{4,8},{8,12},{12,16},{16,20},{20,24},{24,28},{1,5},{5,9},{9,... | collective-permute-start | bytes 36872 | tf_op jit(solution)/shard_map/ppermute | solution.py:22
  125.4 1.3 collective-permute-start.3
  126.7 1.2 convolution_bitcast_fusion.6
  127.9 38.2 %all-reduce.6 = (f32[32,128]{1,0:T(8,128)S(1)}, f32[16,1]{0,1:T(1,128)S(1)}) all-reduce(f32[32,128]{1,0:T(8,128)S(1)} %convolution_bitcast_fusion.6, f32[16,1]{0,1:T(1,128)S(1)} %convolution_bitcast_fusion.7), channel_id=1, replica_groups=mesh['slab'=8,'head'=4] {'slab'}, use_global_device_ids=true, to_apply=%region_9.10 | all-reduce | flops 4112 | bytes 32896 | tf_op jit(solution)/shard_map/psum | solution.py:197
  167.3 1.1 convolution_bitcast_fusion.5
  168.9 66.0 %all-reduce.13.cloned.1.call-done = (f32[4,128,32]{1,2,0:T(8,128)}, f32[128,192]{0,1:T(8,128)}) async-done(((f32[4,128,32]{1,2,0:T(8,128)}, f32[128,192]{0,1:T(8,128)}), (f32[4,128,32]{1,2,0:T(8,128)}, f32[128,192]{0,1:T(8,128)})) %all-reduce.13.cloned.1.call-update) | async-done | bytes 163856 | tf_op jit(solution)/shard_map/psum | solution.py:197
  234.9 1.5 broadcast_multiply_fusion.1
  236.4 1.5 broadcast_multiply_fusion
  (92 shorter events, 7.7 us)
Async XLA Ops:
  7.2 12.8 %copy-start = (bf16[512,16,128]{2,1,0:T(8,128)(2,1)S(1)}, bf16[512,16,128]{2,1,0:T(8,128)(2,1)}, u32[]{:S(2)}) copy-start(bf16[512,16,128]{2,1,0:T(8,128)(2,1)} %param.9) | copy-start | bytes 6291460
  7.2 12.8 %copy-start.22 = (bf16[16,1]{0,1:T(2,128)(2,1)S(1)}, bf16[16,1]{0,1:T(2,128)(2,1)}, u32[]{:S(2)}) copy-start(bf16[16,1]{0,1:T(2,128)(2,1)} %param.13) | copy-start | bytes 100
  7.2 83.5 %all-reduce.11.cloned.1.call-start = ((), (), s32[]{:S(2)}) async-start(), calls=%async_computation | async-start | bytes 524288 | tf_op jit(solution)/shard_map/psum | solution.py:139
  8.5 1.3 copy-start.15
  9.8 7.8 %copy-start.18 = (f32[2,512]{1,0:T(2,128)}, f32[2,512]{1,0:T(2,128)S(1)}, u32[]{:S(2)}) copy-start(f32[2,512]{1,0:T(2,128)S(1)} %add_rsqrt_fusion) | copy-start | bytes 12292
  9.8 10.6 %copy-start.20 = (bf16[32,128]{1,0:T(8,128)(2,1)S(1)}, bf16[32,128]{1,0:T(8,128)(2,1)}, u32[]{:S(2)}) copy-start(bf16[32,128]{1,0:T(8,128)(2,1)} %param.12) | copy-start | bytes 24580
  11.3 17.1 %copy-start.7 = (f32[4,2,512,32]{2,3,0,1:T(8,128)}, f32[4,2,512,32]{2,3,0,1:T(8,128)S(1)}, u32[]{:S(2)}) copy-start(f32[4,2,512,32]{2,3,0,1:T(8,128)S(1)} %get-tuple-element.32) | copy-start | bytes 1572868
  11.4 14.6 %collective-permute-start = (bf16[2,2,48,32]{2,3,0,1:T(8,128)(2,1)S(1)}, bf16[2,2,48,32]{2,3,0,1:T(8,128)(2,1)S(1)}, u32[]{:S(2)}, u32[]{:S(2)}) collective-permute-start(bf16[2,2,48,32]{2,3,0,1:T(8,128)(2,1)S(1)} %get-tuple-element.19), channel_id=1, source_target_pairs={{0,4},{4,8},{8,12},{12,16},{16,20},{20,24},{24,28},{1,5},{5,9},{9,... | collective-permute-start | bytes 36872 | tf_op jit(solution)/shard_map/ppermute | solution.py:22
  16.3 10.4 %collective-permute-start.1 = (bf16[2,2,48,32]{2,3,0,1:T(8,128)(2,1)S(1)}, bf16[2,2,48,32]{2,3,0,1:T(8,128)(2,1)}, u32[]{:S(2)}, u32[]{:S(2)}) collective-permute-start(bf16[2,2,48,32]{2,3,0,1:T(8,128)(2,1)S(1)} %get-tuple-element.20), channel_id=1, source_target_pairs={{4,0},{8,4},{12,8},{16,12},{20,16},{24,20},{28,24},{5,1},{9,5},{13... | collective-permute-start | bytes 36872 | tf_op jit(solution)/shard_map/ppermute | solution.py:24
  18.3 1.5 copy-start.23
  20.0 6.7 %copy-start.10 = (bf16[2,2,512,32]{2,3,0,1:T(8,128)(2,1)S(1)}, bf16[2,2,512,32]{2,3,0,1:T(8,128)(2,1)}, u32[]{:S(2)}) copy-start(bf16[2,2,512,32]{2,3,0,1:T(8,128)(2,1)} %slice.103) | copy-start | bytes 393220
  26.1 0.6 copy-start.17
  35.5 6.0 %copy-start.2 = (bf16[2,2,16,128,32]{3,4,2,1,0:T(8,128)(2,1)}, bf16[2,2,16,128,32]{3,4,2,1,0:T(8,128)(2,1)S(1)}, u32[]{:S(2)}) copy-start(bf16[2,2,16,128,32]{3,4,2,1,0:T(8,128)(2,1)S(1)} %pad_maximum_fusion.1) | copy-start | bytes 1572868
  35.8 0.8 copy-start.6
  37.6 13.8 %copy-start.14 = (bf16[128,128]{1,0:T(8,128)(2,1)S(1)}, bf16[128,128]{1,0:T(8,128)(2,1)}, u32[]{:S(2)}) copy-start(bf16[128,128]{1,0:T(8,128)(2,1)} %all-gather) | copy-start | bytes 98308
  43.4 8.8 %copy-start.1 = (bf16[2,512,128]{2,1,0:T(8,128)(2,1)S(1)}, bf16[2,512,128]{2,1,0:T(8,128)(2,1)}, u32[]{:S(2)}) copy-start(bf16[2,512,128]{2,1,0:T(8,128)(2,1)} %param.8) | copy-start | bytes 786436
  43.4 8.8 %copy-start.11 = (bf16[128,192]{0,1:T(8,128)(2,1)S(1)}, bf16[128,192]{0,1:T(8,128)(2,1)}, u32[]{:S(2)}) copy-start(bf16[128,192]{0,1:T(8,128)(2,1)} %param.14) | copy-start | bytes 147460
  51.4 1.0 copy-start.21
  51.4 1.0 copy-start.24
  51.4 1.0 copy-start.26
  52.4 1.0 copy-start.25
  53.4 0.8 copy-start.12
  55.3 179.6 %all-reduce.13.cloned.1.call-start = ((), (), s32[]{:S(2)}) async-start(), calls=%async_computation.1 | async-start | bytes 327680 | tf_op jit(solution)/shard_map/psum | solution.py:197
  56.4 40.2 %copy-start.3 = (bf16[2,2,16,128,32]{3,4,2,1,0:T(8,128)(2,1)S(1)}, bf16[2,2,16,128,32]{3,4,2,1,0:T(8,128)(2,1)}, u32[]{:S(2)}) copy-start(bf16[2,2,16,128,32]{3,4,2,1,0:T(8,128)(2,1)} %copy-done.2) | copy-start | bytes 1572868
  96.6 1.6 copy-start.5
  96.6 2.0 copy-start.4
  99.6 1.2 copy-start.9
  117.2 9.5 %copy-start.13 = (f32[2,512,32]{1,2,0:T(8,128)S(1)}, f32[2,512,32]{1,2,0:T(8,128)}, u32[]{:S(2)}) copy-start(f32[2,512,32]{1,2,0:T(8,128)} %copy.48) | copy-start | bytes 393220
  118.8 48.0 %copy-start.8 = (bf16[2,16,32,32]{3,2,1,0:T(8,128)(2,1)S(1)}, bf16[2,16,32,32]{3,2,1,0:T(8,128)(2,1)}, u32[]{:S(2)}) copy-start(bf16[2,16,32,32]{3,2,1,0:T(8,128)(2,1)} %fusion.6) | copy-start | bytes 196612
  120.4 46.8 %copy-start.16 = (f32[2,512]{1,0:T(2,128)S(1)}, f32[2,512]{1,0:T(2,128)}, u32[]{:S(2)}) copy-start(f32[2,512]{1,0:T(2,128)} %copy-done.15) | copy-start | bytes 12292
  120.4 46.8 %copy-start.19 = (f32[2,512]{1,0:T(2,128)S(1)}, f32[2,512]{1,0:T(2,128)}, u32[]{:S(2)}) copy-start(f32[2,512]{1,0:T(2,128)} %copy-done.18) | copy-start | bytes 12292
  120.4 46.8 %copy-start.27 = (bf16[1,2,512,32]{2,3,1,0:T(8,128)(2,1)S(1)}, bf16[1,2,512,32]{2,3,1,0:T(8,128)(2,1)}, u32[]{:S(2)}) copy-start(bf16[1,2,512,32]{2,3,1,0:T(8,128)(2,1)} %get-tuple-element.18) | copy-start | bytes 196612
  122.0 44.9 %collective-permute-start.2 = (bf16[2,2,48,32]{2,3,1,0:T(8,128)(2,1)S(1)}, bf16[2,2,48,32]{2,3,1,0:T(8,128)(2,1)S(1)}, u32[]{:S(2)}, u32[]{:S(2)}) collective-permute-start(bf16[2,2,48,32]{2,3,1,0:T(8,128)(2,1)S(1)} %get-tuple-element.21), channel_id=1, source_target_pairs={{0,4},{4,8},{8,12},{12,16},{16,20},{20,24},{24,28},{1,5},{5,9},{9,... | collective-permute-start | bytes 36872 | tf_op jit(solution)/shard_map/ppermute | solution.py:22
  125.4 41.5 %collective-permute-start.3 = (bf16[2,2,48,32]{2,3,1,0:T(8,128)(2,1)S(1)}, bf16[2,2,48,32]{2,3,1,0:T(8,128)(2,1)S(1)}, u32[]{:S(2)}, u32[]{:S(2)}) collective-permute-start(bf16[2,2,48,32]{2,3,1,0:T(8,128)(2,1)S(1)} %get-tuple-element.22), channel_id=1, source_target_pairs={{4,0},{8,4},{12,8},{16,12},{20,16},{24,20},{28,24},{5,1},{9,5},{13... | collective-permute-start | bytes 36872 | tf_op jit(solution)/shard_map/ppermute | solution.py:24
Sparse Core Ops, SparseCore 0:
  55.4 35.2 all-reduce.10
  168.5 66.3 all-reduce.12
where the time goes:
time: 246 us; the launch traced here: 245 us
  waiting for transfers between devices  100 us (41%)
  blocking collectives  49.7 us (20%)
  local copies, waits for them, and re-layouts  28.7 us (12%)
  matrix products  22 us (9%)
  other arithmetic  18.4 us (7%)
  between operations  14.5 us (6%)
  starting transfers between devices  11.1 us (5%)
    psum x1, waiting for transfers between devices, on_device(): lax.psum((grad_proj_local, grad_out_local, grad_pair_local, grad_tok_loca...  66 us
    psum x1, blocking collectives, on_device(): lax.psum((grad_proj_local, grad_out_local, grad_pair_local, grad_tok_loca...  38.2 us
    psum x1, waiting for transfers between devices, on_device(): mixed_grad = lax.psum(mixed_terms.astype(jnp.bfloat16), 'head')  34.3 us
    slice x4, local copies, waits for them, and re-layouts, key_unwindowed_rows(): windowed[..., Q_WIN * offset:Q_WIN * (offset + 1), :]  8.83 us
    reshape x4, local copies, waits for them, and re-layouts, key_unwindowed_rows(): windowed[..., Q_WIN * offset:Q_WIN * (offset + 1), :]  8.59 us
    ppermute x2, starting transfers between devices, extended_2(): lax.ppermute(tail, axis, [(i, (i + 1) % count) for i in range(ends)])  8.23 us
    all_gather x1, blocking collectives, on_device(): lax.all_gather(heads_out[None], 'head', axis=0, tiled=True)  5.85 us
    all_gather x1, blocking collectives, on_device(): lax.all_gather(w_out[None], 'head', axis=0, tiled=True)  5.64 us
  transfers between devices with their start and end apart: 6, of which 2 were waited for; matrix products, arithmetic and copies ran while one was open for 2% of the time, Pallas kernels for 0%

commit v1 on v0

v1 whole, which is shorter than its diff:
```python
import functools
import jax
import jax.numpy as jnp
from jax import lax
from jax.experimental import pallas as pl
from jax.experimental.pallas import tpu as pltpu
from jax.sharding import PartitionSpec as P

Q_WIN = 32
K_WIN = 128
RIM = 48
EPSILON = 1e-05
MASKED = -1e30
BF = jnp.bfloat16
F32 = jnp.float32
NT = (((1,), (1,)), ((), ()))
NN = (((1,), (0,)), ((), ()))
TN = (((0,), (0,)), ((), ()))


def mm(a, b, dims=NN):
    return lax.dot_general(a, b, dims, preferred_element_type=F32)


def iota(shape, dim):
    return lax.broadcasted_iota(jnp.int32, shape, dim)


def layer_norm(x):
    x = x.astype(F32)
    centered = x - jnp.mean(x, axis=-1, keepdims=True)
    variance = jnp.mean(centered * centered, axis=-1, keepdims=True)
    return (centered * lax.rsqrt(variance + EPSILON)).astype(BF)


def kernel(
    n, heads, inner,
    feats, pair_any, slot, wproj, wout, wpair, wtok, dtok,
    tok_out, gproj_out, gout_out, gpair_out, gtok_out,
    pair, halo, nx, wo, wbig, bdqg, bdk, bdv, bias, ncat, gate, qp, ucat, prob, zcat, att,
    hbuf, mhs, acts, ags, mtc, og0, osend, orecv, agp, ggp, qgp, ycat,
    gosend, gorecv, ebuf, erecv, eres, lbuf, lrecv, precv, lres, xbuf,
    pair_sem, halo_sem, wo_sem, h_sem, o_sem, go_sem, e_sem, eg_sem, l_sem, lp_sem, lg_sem, x_sem,
):
    samples, atoms, width = feats.shape
    depth = wproj.shape[2]
    lanes = width
    groups = lanes // depth
    step = groups * Q_WIN
    chunks = atoms // step
    rows = samples * Q_WIN
    slots = dtok.shape[1]
    channels = wpair.shape[0]
    token_cols = wtok.shape[1]
    scale = depth ** (-0.5)
    factor = (samples * atoms * n) ** (-0.5)
    outer = n // inner
    me_s = lax.axis_index("slab")
    me_h = lax.axis_index("head")
    own = lax.rem(me_s, inner)
    base = me_s - own
    sends = []

    def head_peer(k):
        return {"head": lax.rem(me_h + k + heads, heads)}

    def inner_peer(k):
        return {"slab": base + lax.rem(own + k, inner)}

    def outer_peer(k):
        return {"slab": lax.rem(me_s + k * inner, n)}

    def ring_peer(k):
        return {"slab": lax.rem(me_s + k + n, n)}

    def send(src, dst, sems, index, device):
        copy = pltpu.make_async_remote_copy(
            src_ref=src, dst_ref=dst, send_sem=sems.at[(0,) + index], recv_sem=sems.at[(1,) + index],
            device_id=device, device_id_type=pl.DeviceIdType.MESH,
        )
        copy.start()
        sends.append(copy)
        return copy

    pair_copy = pltpu.make_async_copy(pair_any, pair, pair_sem)
    pair_copy.start()
    greeted = [head_peer(k) for k in range(1, heads)] + [inner_peer(k) for k in range(1, inner)]
    greeted += [outer_peer(k) for k in range(1, outer)]
    if outer > 1:
        greeted += [ring_peer(1), ring_peer(-1)]
    barrier = pltpu.get_barrier_semaphore()
    for device in greeted:
        pl.semaphore_signal(barrier, inc=1, device_id=device, device_id_type=pl.DeviceIdType.MESH)

    for s in range(samples):
        nx[s, RIM : RIM + atoms, :] = layer_norm(feats[s])
    lane_group = iota((lanes, lanes), 1) // depth
    row_group = iota((lanes, lanes), 0) // depth
    spreader = (lax.rem(iota((depth, lanes), 1), depth) == iota((depth, lanes), 0)).astype(F32).astype(BF)
    wide = [mm(wproj[f], spreader) for f in range(4)]
    for g in range(groups):
        keep = lane_group == g
        span = slice(g * lanes, (g + 1) * lanes)
        bdqg[span, :lanes] = jnp.where(keep, wide[0], 0.0).astype(BF)
        bdqg[span, lanes:] = jnp.where(keep, wide[3], 0.0).astype(BF)
        bdk[span, :] = jnp.where(keep, wide[1], 0.0).astype(BF)
        bdv[span, :] = jnp.where(keep, wide[2], 0.0).astype(BF)
    wo[0] = wout[...]

    pl.semaphore_wait(barrier, len(greeted))

    to_left = send(feats.at[:, 0:RIM, :], halo.at[1], halo_sem, (1,), ring_peer(-1))
    to_right = send(feats.at[:, atoms - RIM : atoms, :], halo.at[0], halo_sem, (0,), ring_peer(1))
    wo_copies = [send(wout, wo.at[k], wo_sem, (k - 1,), head_peer(k)) for k in range(1, heads)]

    for c in range(chunks):
        for s in range(samples):
            for g in range(groups):
                at = RIM + c * step + g * Q_WIN
                ncat[c * rows + s * Q_WIN : c * rows + (s + 1) * Q_WIN, g * lanes : (g + 1) * lanes] = nx[
                    s, at : at + Q_WIN, :
                ]
    projected = mm(ncat[...], bdqg[...])
    queries = (projected[:, :lanes] * scale).astype(BF)
    qp[...] = queries
    gate[...] = jax.nn.sigmoid(projected[:, lanes:])
    ucat[...] = mm(queries, bdk[...], NT).astype(BF)

    slot_ids = me_s * slots + iota((slots, atoms), 0)
    member = jnp.where(slot[...] == slot_ids, 1.0, 0.0)
    divisor = jnp.maximum(jnp.sum(member, axis=1, keepdims=True), 1.0)
    member = member.astype(BF)
    tok_grad = [(dtok[s].astype(F32) / divisor).astype(BF) for s in range(samples)]

    flat = Q_WIN * channels
    picker = lax.rem(iota((channels, flat), 1), channels) == iota((channels, flat), 0)
    w_wide = jnp.broadcast_to(wpair[...].astype(F32), (channels, Q_WIN)).astype(BF)
    w_rows = mm(w_wide, picker.astype(F32).astype(BF), TN)
    diagonal = iota((Q_WIN, flat), 1) // channels == iota((Q_WIN, flat), 0)
    mixer = jnp.where(diagonal, w_rows, 0.0).astype(BF)
    pair_copy.wait()
    for b in range(chunks * groups):
        bias[b] = mm(mixer, pair[b * flat : (b + 1) * flat, :])

    for k in range(heads):
        if k:
            wo_copies[k - 1].wait_recv()
        tall = jnp.concatenate([wo[k]] * groups, axis=0).astype(F32)
        for g in range(groups):
            wbig[k * lanes : (k + 1) * lanes, g * lanes : (g + 1) * lanes] = jnp.where(
                row_group == g, tall, 0.0
            ).astype(BF)

    to_right.wait_recv()
    to_left.wait_recv()
    for s in range(samples):
        nx[s, 0:RIM, :] = layer_norm(halo[0, s])
        nx[s, RIM + atoms : RIM + atoms + RIM, :] = layer_norm(halo[1, s])

    h_copies, o_copies = {}, {}

    def forward(c):
        at_rows = slice(c * rows, (c + 1) * rows)
        for s in range(samples):
            for g in range(groups):
                b = c * groups + g
                cols = slice(g * lanes, (g + 1) * lanes)
                here = slice(c * rows + s * Q_WIN, c * rows + (s + 1) * Q_WIN)
                window = nx[s, b * Q_WIN : b * Q_WIN + K_WIN, :]
                scores = mm(ucat[here, cols], window, NT) + bias[b]
                first = b * Q_WIN - RIM
                if first < 0 or first + K_WIN > atoms:
                    where = me_s * atoms + first + iota((Q_WIN, K_WIN), 1)
                    scores = jnp.where((where >= 0) & (where < atoms * n), scores, MASKED)
                top = jnp.max(scores, axis=1, keepdims=True)
                e = jnp.exp(scores - top)
                p = e / jnp.sum(e, axis=1, keepdims=True)
                prob[s, b] = p
                zcat[here, cols] = mm(p.astype(BF), window).astype(BF)
        attended = mm(zcat[at_rows, :], bdv[...])
        att[at_rows, :] = attended
        hbuf[0, c] = (gate[at_rows, :] * attended).astype(BF)
        h_copies[c] = [
            send(hbuf.at[0, c], hbuf.at[k, c], h_sem, (k - 1, c), head_peer(k)) for k in range(1, heads)
        ]

    def middle(c):
        for copy in h_copies[c]:
            copy.wait_recv()
        mixed = mm(jnp.concatenate([hbuf[k, c] for k in range(heads)], axis=1), wbig[...])
        for s in range(samples):
            parts = [mixed[s * Q_WIN : (s + 1) * Q_WIN, g * lanes : (g + 1) * lanes] for g in range(groups)]
            span = slice(c * step, (c + 1) * step)
            half = (feats[s, span, :].astype(F32) + jnp.concatenate(parts, axis=0)).astype(BF)
            mhs[s, span, :] = half
            pre = mm(half, wtok[...])
            g1 = jax.nn.sigmoid(pre)
            acts[s, span, :] = (pre * g1).astype(BF)
            spread = mm(member[:, span], tok_grad[s], TN)
            ag = (spread * (g1 * (1.0 + pre * (1.0 - g1)))).astype(BF)
            ags[s, span, :] = ag
            mt = mm(ag, wtok[...], NT).astype(BF)
            for g in range(groups):
                mtc[c * rows + s * Q_WIN : c * rows + (s + 1) * Q_WIN, g * lanes : (g + 1) * lanes] = mt[
                    g * Q_WIN : (g + 1) * Q_WIN, :
                ]
        og = mm(mtc[c * rows : (c + 1) * rows, :], wbig[...], NT)
        og0[c] = og[:, :lanes]
        o_copies[c] = []
        for k in range(1, heads):
            osend[k - 1, c] = og[:, k * lanes : (k + 1) * lanes].astype(BF)
            o_copies[c].append(send(osend.at[k - 1, c], orecv.at[k - 1, c], o_sem, (k - 1, c), head_peer(-k)))

    def diagonal_sum(a):
        total = a[0:depth, 0:lanes]
        for g in range(1, groups):
            total = total + a[g * depth : (g + 1) * depth, g * lanes : (g + 1) * lanes]
        return total

    pair_terms = [None]

    def backward(c):
        at_rows = slice(c * rows, (c + 1) * rows)
        for copy in o_copies[c]:
            copy.wait_recv()
        og = og0[c]
        for k in range(1, heads):
            og = og + orecv[k - 1, c].astype(F32)
        gt = gate[at_rows, :]
        ag = (gt * og).astype(BF)
        agp[at_rows, :] = ag
        ggp[at_rows, :] = (og * att[at_rows, :] * gt * (1.0 - gt)).astype(BF)
        tcat = mm(ag, bdv[...], NT).astype(BF)
        for g in range(groups):
            b = c * groups + g
            cols = slice(g * lanes, (g + 1) * lanes)
            both = None
            for s in range(samples):
                here = slice(c * rows + s * Q_WIN, c * rows + (s + 1) * Q_WIN)
                window = nx[s, b * Q_WIN : b * Q_WIN + K_WIN, :]
                dp = mm(tcat[s * Q_WIN : (s + 1) * Q_WIN, cols], window, NT)
                p = prob[s, b]
                ds = (p * (dp - jnp.sum(p * dp, axis=1, keepdims=True))).astype(BF)
                ycat[here, cols] = mm(ds, window).astype(BF)
                ds = ds.astype(F32)
                both = ds if both is None else both + ds
            term = mm(both.astype(BF), pair[b * flat : (b + 1) * flat, :], NT)
            pair_terms[0] = term if pair_terms[0] is None else pair_terms[0] + term
        qgp[at_rows, :] = (scale * mm(ycat[at_rows, :], bdk[...])).astype(BF)

    order = []
    for t in range(chunks + 3):
        if t < chunks:
            order.append((forward, t))
        if 0 <= t - 1 < chunks:
            order.append((middle, t - 1))
        if t - 3 >= 0:
            order.append((backward, t - 3))
    late = [entry for entry in order if entry[0] is backward][1:]
    for step_of, c in [entry for entry in order if entry not in late]:
        step_of(c)

    hcat = jnp.concatenate(
        [jnp.concatenate([hbuf[k, c] for c in range(chunks)], axis=0) for k in range(heads)], axis=1
    )
    go_copies = []
    cross = mm(hcat, mtc[...], TN)
    go_own = diagonal_sum(cross[0:lanes])
    for k in range(1, heads):
        gosend[k - 1] = diagonal_sum(cross[k * lanes : (k + 1) * lanes]).astype(BF)
        go_copies.append(send(gosend.at[k - 1], gorecv.at[k - 1], go_sem, (k - 1,), head_peer(-k)))

    gtok = None
    for s in range(samples):
        sums = mm(member, acts[s])
        tok_out[s] = (sums / divisor).astype(BF)
        term = mm(ags[s], mhs[s], TN)
        gtok = term if gtok is None else gtok + term

    half_late = len(late) // 2
    for step_of, c in late[:half_late]:
        step_of(c)

    def exchange_outer(value, where):
        if outer == 1:
            return value
        xbuf[where, 0, : value.shape[0], :] = value.astype(BF)
        copies = [
            send(xbuf.at[where, 0], xbuf.at[where, k], x_sem, (where, k - 1), outer_peer(k)) for k in range(1, outer)
        ]
        for k in range(1, outer):
            copies[k - 1].wait_recv()
            value = value + xbuf[where, k, : value.shape[0], :].astype(F32)
        return value

    def scatter(buf, recv, sems):
        return [
            send(buf.at[lax.rem(own + k, inner)], recv.at[k - 1], sems, (k - 1,), inner_peer(k))
            for k in range(1, inner)
        ]

    def total_of(copies, value, recv):
        for k in range(1, inner):
            copies[k - 1].wait_recv()
            value = value + recv[k - 1].astype(F32)
        return value

    def gather(res, value, sems):
        res[own] = value.astype(BF)
        return [send(res.at[own], res.at[own], sems, (k - 1,), inner_peer(k)) for k in range(1, inner)]

    for k in range(1, heads):
        go_copies[k - 1].wait_recv()
        go_own = go_own + gorecv[k - 1].astype(F32)
    piece = ebuf.shape[1]
    parts = [gtok, go_own]
    spare = inner * piece - token_cols - depth
    if spare:
        parts.append(jnp.zeros((spare, lanes), F32))
    e_rows = jnp.concatenate(parts, axis=0).astype(BF)
    for j in range(inner):
        ebuf[j] = e_rows[j * piece : (j + 1) * piece]
    e_copies = scatter(ebuf, erecv, e_sem)

    for step_of, c in late[half_late:]:
        step_of(c)

    l_rows = jnp.concatenate(
        [
            diagonal_sum(mm(qgp[...], ncat[...], TN)),
            diagonal_sum(mm(qp[...], ycat[...], TN)),
            diagonal_sum(mm(agp[...], zcat[...], TN)),
            diagonal_sum(mm(ggp[...], ncat[...], TN)),
        ],
        axis=0,
    ).astype(BF)
    piece = lbuf.shape[1]
    for j in range(inner):
        lbuf[j] = l_rows[j * piece : (j + 1) * piece]
    l_copies = scatter(lbuf, lrecv, l_sem)
    pair_row = jnp.sum(jnp.where(diagonal, pair_terms[0], 0.0), axis=0, keepdims=True)
    pair_own = jnp.sum(jnp.where(picker, pair_row, 0.0), axis=1, keepdims=True)
    pair_own = jnp.broadcast_to(pair_own, (channels, lanes))
    precv[0] = pair_own.astype(BF)
    p_copies = [send(precv.at[0], precv.at[k], lp_sem, (k - 1,), inner_peer(k)) for k in range(1, inner)]

    total = exchange_outer(total_of(e_copies, ebuf[own].astype(F32), erecv), 0)
    eg_copies = gather(eres, total, eg_sem)
    total = exchange_outer(total_of(l_copies, lbuf[own].astype(F32), lrecv), 1)
    lg_copies = gather(lres, total, lg_sem)
    for k in range(1, inner):
        p_copies[k - 1].wait_recv()
        pair_own = pair_own + precv[k].astype(F32)
    pair_own = exchange_outer(pair_own, 2)
    gpair_out[...] = pair_own[:, 0:1] * factor

    def arrived(copies, res):
        for k in range(1, inner):
            copies[k - 1].wait_recv()
        return jnp.concatenate([res[j] for j in range(inner)], axis=0).astype(F32) * factor

    whole = arrived(eg_copies, eres)
    gtok_out[...] = whole[0:token_cols].T
    gout_out[...] = whole[token_cols : token_cols + depth]
    whole = arrived(lg_copies, lres)
    for f in range(4):
        gproj_out[f] = whole[f * depth : (f + 1) * depth].T
    for copy in sends:
        copy.wait_send()


def on_device(atom_feats, pair_feats, tok_slot, w_proj, w_out, w_pair, w_tok, d_tok):
    samples, atoms, width = atom_feats.shape
    depth = w_proj.shape[2]
    lanes = width
    groups = lanes // depth
    step = groups * Q_WIN
    chunks = atoms // step
    rows = samples * Q_WIN
    blocks = chunks * groups
    slots, token_cols = d_tok.shape[1], d_tok.shape[2]
    channels = w_pair.shape[0]
    n = lax.axis_size("slab")
    heads = lax.axis_size("head")
    inner = next(m for m in (8, 4, 2, 1) if n % m == 0)
    outer = n // inner
    e_piece = -(-(token_cols + depth) // (16 * inner)) * 16
    l_piece = -(-(4 * depth) // (16 * inner)) * 16
    peers = max(inner - 1, 1)
    far = max(outer - 1, 1)

    def vm(*shape, dtype=BF):
        return pltpu.VMEM(shape, dtype)

    def sems(*shape):
        return pltpu.SemaphoreType.DMA((2,) + shape)

    packed = chunks * rows
    scratch = [
        vm(atoms * channels, K_WIN),
        vm(2, samples, RIM, width),
        vm(samples, atoms + 2 * RIM, width),
        vm(heads, depth, width),
        vm(heads * lanes, groups * lanes),
        vm(groups * lanes, 2 * lanes),
        vm(groups * lanes, lanes),
        vm(groups * lanes, lanes),
        vm(blocks, Q_WIN, K_WIN, dtype=F32),
        vm(packed, groups * lanes),
        vm(packed, lanes, dtype=F32),
        vm(packed, lanes),
        vm(packed, groups * lanes),
        vm(samples, blocks, Q_WIN, K_WIN, dtype=F32),
        vm(packed, groups * lanes),
        vm(packed, lanes, dtype=F32),
        vm(heads, chunks, rows, lanes),
        vm(samples, atoms, width),
        vm(samples, atoms, token_cols),
        vm(samples, atoms, token_cols),
        vm(packed, groups * lanes),
        vm(chunks, rows, lanes, dtype=F32),
        vm(heads - 1, chunks, rows, lanes),
        vm(heads - 1, chunks, rows, lanes),
        vm(packed, lanes),
        vm(packed, lanes),
        vm(packed, lanes),
        vm(packed, groups * lanes),
        vm(heads - 1, depth, lanes),
        vm(heads - 1, depth, lanes),
        vm(inner, e_piece, lanes),
        vm(peers, e_piece, lanes),
        vm(inner, e_piece, lanes),
        vm(inner, l_piece, lanes),
        vm(peers, l_piece, lanes),
        vm(inner, channels, lanes),
        vm(inner, l_piece, lanes),
        vm(3, outer, max(e_piece, l_piece, channels), lanes),
        pltpu.SemaphoreType.DMA,
        sems(2),
        sems(heads - 1),
        sems(heads - 1, chunks),
        sems(heads - 1, chunks),
        sems(heads - 1),
        sems(peers),
        sems(peers),
        sems(peers),
        sems(peers),
        sems(peers),
        sems(3, far),
    ]
    in_vmem = pl.BlockSpec(memory_space=pltpu.VMEM)
    return pl.pallas_call(
        functools.partial(kernel, n, heads, inner),
        out_shape=(
            jax.ShapeDtypeStruct((samples, slots, token_cols), BF),
            jax.ShapeDtypeStruct((4, width, depth), F32),
            jax.ShapeDtypeStruct((depth, width), F32),
            jax.ShapeDtypeStruct((channels, 1), F32),
            jax.ShapeDtypeStruct((width, token_cols), F32),
        ),
        in_specs=[in_vmem, pl.BlockSpec(memory_space=pl.ANY)] + [in_vmem] * 6,
        out_specs=[in_vmem] * 5,
        scratch_shapes=scratch,
        compiler_params=pltpu.CompilerParams(
            collective_id=0, has_side_effects=True, vmem_limit_bytes=48 * 1024 * 1024
        ),
    )(
        atom_feats,
        pair_feats.reshape(atoms * channels, K_WIN),
        tok_slot.reshape(1, atoms),
        w_proj,
        w_out,
        w_pair,
        w_tok,
        d_tok,
    )


def solution(mesh):
    return jax.shard_map(
        on_device,
        mesh=mesh,
        in_specs=(
            P(None, "slab", None),
            P("slab", None, None),
            P("slab"),
            P(None, None, "head"),
            P("head", None),
            P(None, "head"),
            P(None, "head"),
            P(None, "slab", "head"),
        ),
        out_specs=(
            P(None, "slab", "head"),
            P(None, None, "head"),
            P("head", None),
            P(None, "head"),
            P(None, "head"),
        ),
        check_vma=False,
    )
```

time: 246 us -> 55.9 us (0.23)
  waiting for transfers between devices: 100 us -> 0 us
  blocking collectives: 49.7 us -> 0 us
  Pallas kernels: 0 us -> 44.3 us
  matrix products: 22 us -> 0 us
  other arithmetic: 18.4 us -> 0 us
  local copies, waits for them, and re-layouts: 28.7 us -> 10.5 us
  between operations: 14.5 us -> 0.67 us
  starting transfers between devices: 11.1 us -> 0 us
    psum x2 -> x0, waiting for transfers between devices: 100 us -> none  [the longest x1 66 us: on_device(): lax.psum((grad_proj_local, grad_out_local, grad_pair_local, grad_tok_loca...]
    pallas_call x0 -> x1, Pallas kernels: none -> 44.3 us  [on_device(): pl.pallas_call(functools.partial(kernel, n, heads, inner), out_shape=(jax...]
    psum x1 -> x0, blocking collectives: 38.2 us -> none  [on_device(): lax.psum((grad_proj_local, grad_out_local, grad_pair_local, grad_tok_loca...]
    dot_general x18 -> x0, matrix products: 22 us -> none  [the longest x1 3.85 us: on_device(): jnp.einsum('sbqk,sbkd->sbqd', weight_half_precision, value_window_rows, p...]
    reshape x15 -> x0, local copies, waits for them, and re-layouts: 16.9 us -> none  [the longest x4 8.59 us: key_unwindowed_rows(): windowed[..., Q_WIN * offset:Q_WIN * (offset + 1), :]]
    all_gather x2 -> x0, blocking collectives: 11.5 us -> none  [the longest x1 5.85 us: on_device(): lax.all_gather(heads_out[None], 'head', axis=0, tiled=True)]
    ppermute x4 -> x0, starting transfers between devices: 10.8 us -> none  [the longest x2 8.23 us: extended_2(): lax.ppermute(tail, axis, [(i, (i + 1) % count) for i in range(ends)])]
    slice x7 -> x0, local copies, waits for them, and re-layouts: 9.07 us -> none  [the longest x4 8.83 us: key_unwindowed_rows(): windowed[..., Q_WIN * offset:Q_WIN * (offset + 1), :]]
  transfers between devices with their start and end apart: 6 -> 0, of which waited for: 2 -> 0; matrix products, arithmetic and copies ran while one was open for 2% -> 0% of each run, Pallas kernels for 0% -> 0%
where the time goes in v1:
time: 55.9 us; the launch traced here: 55.4 us
  Pallas kernels  44.3 us (79%)
  local copies, waits for them, and re-layouts  10.5 us (19%)
  between operations  0.67 us (1%)
    pallas_call x1, Pallas kernels, on_device(): pl.pallas_call(functools.partial(kernel, n, heads, inner), out_shape=(jax...  44.3 us
    unnamed x15, local copies, waits for them, and re-layouts  8.41 us
    pallas_call x3, local copies, waits for them, and re-layouts, on_device(): pl.pallas_call(functools.partial(kernel, n, heads, inner), out_shape=(jax...  2.06 us

profile of v1, /device:TPU:0, one launch (start us, length us, event | category | flops | bytes accessed | tf_op | source)
XLA Modules:
  0.0 55.4 jit_solution(18283749120778329920)
XLA Ops:
  0.6 0.7 %copy.14.wpair = bf16[16,1]{1,0:T(8,128)(2,1)S(1)} copy(bf16[16,1]{0,1:T(2,128)(2,1)} %param.13) | data formatting | bytes 64 | tf_op args[5]
  1.4 0.9 %copy.15.wtok = bf16[128,192]{1,0:T(8,128)(2,1)S(1)} copy(bf16[128,192]{0,1:T(8,128)(2,1)} %param.14) | data formatting | bytes 98304 | tf_op args[6]
  2.3 0.9 %copy.13.wproj = bf16[4,128,32]{2,1,0:T(8,128)(2,1)S(1)} copy(bf16[4,128,32]{1,2,0:T(8,128)(2,1)} %param.11) | data formatting | bytes 65536 | tf_op args[3]
  3.2 0.0 copy-start
  3.2 1.6 %copy-done = bf16[512,16,128]{2,1,0:T(8,128)(2,1)S(1)} copy-done((bf16[512,16,128]{2,1,0:T(8,128)(2,1)S(1)}, bf16[512,16,128]{2,1,0:T(8,128)(2,1)}, u32[]{:S(2)}) %copy-start) | copy-done | bytes 2097176
  4.8 0.0 copy-start.1
  4.8 0.9 %copy-done.1 = bf16[2,512,128]{2,1,0:T(8,128)(2,1)S(1)} copy-done((bf16[2,512,128]{2,1,0:T(8,128)(2,1)S(1)}, bf16[2,512,128]{2,1,0:T(8,128)(2,1)}, u32[]{:S(2)}) %copy-start.1) | copy-done | bytes 262168
  5.7 0.0 copy-start.2
  5.7 0.8 %copy-done.2 = bf16[2,32,192]{2,1,0:T(8,128)(2,1)S(1)} copy-done((bf16[2,32,192]{2,1,0:T(8,128)(2,1)S(1)}, bf16[2,32,192]{2,1,0:T(8,128)(2,1)}, u32[]{:S(2)}) %copy-start.2) | copy-done | bytes 24600
  6.5 0.0 copy-start.3
  6.5 0.7 %copy-done.3 = bf16[32,128]{1,0:T(8,128)(2,1)S(1)} copy-done((bf16[32,128]{1,0:T(8,128)(2,1)S(1)}, bf16[32,128]{1,0:T(8,128)(2,1)}, u32[]{:S(2)}) %copy-start.3) | copy-done | bytes 8216
  7.2 0.0 copy-start.4
  7.2 0.7 %copy-done.4 = s32[512]{0:T(512)S(1)} copy-done((s32[512]{0:T(512)S(1)}, s32[512]{0:T(512)}, u32[]{:S(2)}) %copy-start.4) | copy-done | bytes 2072
  7.8 44.3 %shard_map.119 = (bf16[2,32,192]{2,1,0:T(8,128)(2,1)S(1)}, f32[4,128,32]{2,1,0:T(8,128)S(1)}, f32[32,128]{1,0:T(8,128)S(1)}, f32[16,1]{1,0:T(8,128)S(1)}, f32[128,192]{1,0:T(8,128)S(1)}) custom-call(bf16[2,512,128]{2,1,0:T(8,128)(2,1)S(1)} %copy-done.1, bf16[8192,128]{1,0:T(8,128)(2,1)S(1)} %bitcast.2, s32[1,512]{1,0:T(1,128)S(1)} %bitcast.3, ...), custom_call_target="tpu_custom_call" | custom-call | tf_op jit(solution)/shard_map/pallas_call | solution.py:452
  52.1 0.6 %copy.17 = f32[16,1]{0,1:T(1,128)} copy(f32[16,1]{1,0:T(8,128)S(1)} %get-tuple-element.8) | data formatting | bytes 128 | tf_op jit(solution)/shard_map/pallas_call | solution.py:452
  52.7 0.7 %copy.16 = f32[4,128,32]{1,2,0:T(8,128)} copy(f32[4,128,32]{2,1,0:T(8,128)S(1)} %get-tuple-element.6) | data formatting | bytes 131072 | tf_op jit(solution)/shard_map/pallas_call | solution.py:452
  53.5 0.7 %copy.18 = f32[128,192]{0,1:T(8,128)} copy(f32[128,192]{1,0:T(8,128)S(1)} %get-tuple-element.9) | data formatting | bytes 196608 | tf_op jit(solution)/shard_map/pallas_call | solution.py:452
  54.2 0.6 %copy.21 = bf16[2,32,192]{2,1,0:T(8,128)(2,1)} copy(bf16[2,32,192]{2,1,0:T(8,128)(2,1)S(1)} %get-tuple-element.15) | data formatting | bytes 49152
  54.8 0.6 %copy.22 = f32[32,128]{1,0:T(8,128)} copy(f32[32,128]{1,0:T(8,128)S(1)} %get-tuple-element.17) | data formatting | bytes 32768
Async XLA Ops:
  3.2 1.6 %copy-start = (bf16[512,16,128]{2,1,0:T(8,128)(2,1)S(1)}, bf16[512,16,128]{2,1,0:T(8,128)(2,1)}, u32[]{:S(2)}) copy-start(bf16[512,16,128]{2,1,0:T(8,128)(2,1)} %param.9) | copy-start | bytes 6291460
  4.8 0.9 %copy-start.1 = (bf16[2,512,128]{2,1,0:T(8,128)(2,1)S(1)}, bf16[2,512,128]{2,1,0:T(8,128)(2,1)}, u32[]{:S(2)}) copy-start(bf16[2,512,128]{2,1,0:T(8,128)(2,1)} %feats.1) | copy-start | bytes 786436
  5.7 0.8 %copy-start.2 = (bf16[2,32,192]{2,1,0:T(8,128)(2,1)S(1)}, bf16[2,32,192]{2,1,0:T(8,128)(2,1)}, u32[]{:S(2)}) copy-start(bf16[2,32,192]{2,1,0:T(8,128)(2,1)} %dtok.1) | copy-start | bytes 73732
  6.5 0.7 %copy-start.3 = (bf16[32,128]{1,0:T(8,128)(2,1)S(1)}, bf16[32,128]{1,0:T(8,128)(2,1)}, u32[]{:S(2)}) copy-start(bf16[32,128]{1,0:T(8,128)(2,1)} %wout.1) | copy-start | bytes 24580
  7.2 0.7 %copy-start.4 = (s32[512]{0:T(512)S(1)}, s32[512]{0:T(512)}, u32[]{:S(2)}) copy-start(s32[512]{0:T(512)} %param.10) | copy-start | bytes 6148

commit v2 on v1

--- a/solution.py
+++ b/solution.py
@@ -35,23 +35,23 @@
 
 def kernel(
     n, heads, inner,
-    feats, pair_any, slot, wproj, wout, wpair, wtok, dtok,
+    feats_in, pair_in, slot_in, wproj_in, wout_in, wpair_in, wtok_in, dtok_in,
     tok_out, gproj_out, gout_out, gpair_out, gtok_out,
-    pair, halo, nx, wo, wbig, bdqg, bdk, bdv, bias, ncat, gate, qp, ucat, prob, zcat, att,
+    feats, pair, slot, wproj, wout, wpair, wtok, dtok, halo, nx, wo, wbig, bdqg, bdk, bdv, bias, ncat, gate, qp, ucat, prob, zcat, att,
     hbuf, mhs, acts, ags, mtc, og0, osend, orecv, agp, ggp, qgp, ycat,
     gosend, gorecv, ebuf, erecv, eres, lbuf, lrecv, precv, lres, xbuf,
-    pair_sem, halo_sem, wo_sem, h_sem, o_sem, go_sem, e_sem, eg_sem, l_sem, lp_sem, lg_sem, x_sem,
+    in_sem, halo_sem, wo_sem, h_sem, o_sem, go_sem, e_sem, eg_sem, l_sem, lp_sem, lg_sem, x_sem,
 ):
     samples, atoms, width = feats.shape
-    depth = wproj.shape[2]
+    depth = wproj.shape[1]
     lanes = width
     groups = lanes // depth
     step = groups * Q_WIN
     chunks = atoms // step
     rows = samples * Q_WIN
     slots = dtok.shape[1]
-    channels = wpair.shape[0]
-    token_cols = wtok.shape[1]
+    channels = wpair.shape[1]
+    token_cols = wtok.shape[0]
     scale = depth ** (-0.5)
     factor = (samples * atoms * n) ** (-0.5)
     outer = n // inner
@@ -82,8 +82,11 @@
         sends.append(copy)
         return copy
 
-    pair_copy = pltpu.make_async_copy(pair_any, pair, pair_sem)
-    pair_copy.start()
+    ins = (feats_in, wproj_in, wout_in, slot_in, dtok_in, wpair_in, wtok_in, pair_in)
+    kept = (feats, wproj, wout, slot, dtok, wpair, wtok, pair)
+    loads = [pltpu.make_async_copy(a, b, in_sem.at[i]) for i, (a, b) in enumerate(zip(ins, kept))]
+    for load in loads:
+        load.start()
     greeted = [head_peer(k) for k in range(1, heads)] + [inner_peer(k) for k in range(1, inner)]
     greeted += [outer_peer(k) for k in range(1, outer)]
     if outer > 1:
@@ -92,12 +95,15 @@
     for device in greeted:
         pl.semaphore_signal(barrier, inc=1, device_id=device, device_id_type=pl.DeviceIdType.MESH)
 
+    loads[0].wait()
     for s in range(samples):
         nx[s, RIM : RIM + atoms, :] = layer_norm(feats[s])
+    loads[1].wait()
+    loads[2].wait()
     lane_group = iota((lanes, lanes), 1) // depth
     row_group = iota((lanes, lanes), 0) // depth
     spreader = (lax.rem(iota((depth, lanes), 1), depth) == iota((depth, lanes), 0)).astype(F32).astype(BF)
-    wide = [mm(wproj[f], spreader) for f in range(4)]
+    wide = [mm(wproj[f], spreader, TN) for f in range(4)]
     for g in range(groups):
         keep = lane_group == g
         span = slice(g * lanes, (g + 1) * lanes)
@@ -126,6 +132,8 @@
     gate[...] = jax.nn.sigmoid(projected[:, lanes:])
     ucat[...] = mm(queries, bdk[...], NT).astype(BF)
 
+    for i in (3, 4, 5, 6):
+        loads[i].wait()
     slot_ids = me_s * slots + iota((slots, atoms), 0)
     member = jnp.where(slot[...] == slot_ids, 1.0, 0.0)
     divisor = jnp.maximum(jnp.sum(member, axis=1, keepdims=True), 1.0)
@@ -134,11 +142,11 @@
 
     flat = Q_WIN * channels
     picker = lax.rem(iota((channels, flat), 1), channels) == iota((channels, flat), 0)
-    w_wide = jnp.broadcast_to(wpair[...].astype(F32), (channels, Q_WIN)).astype(BF)
-    w_rows = mm(w_wide, picker.astype(F32).astype(BF), TN)
+    w_wide = jnp.broadcast_to(wpair[...].astype(F32), (Q_WIN, channels)).astype(BF)
+    w_rows = mm(w_wide, picker.astype(F32).astype(BF))
     diagonal = iota((Q_WIN, flat), 1) // channels == iota((Q_WIN, flat), 0)
     mixer = jnp.where(diagonal, w_rows, 0.0).astype(BF)
-    pair_copy.wait()
+    loads[7].wait()
     for b in range(chunks * groups):
         bias[b] = mm(mixer, pair[b * flat : (b + 1) * flat, :])
 
@@ -193,13 +201,13 @@
             span = slice(c * step, (c + 1) * step)
             half = (feats[s, span, :].astype(F32) + jnp.concatenate(parts, axis=0)).astype(BF)
             mhs[s, span, :] = half
-            pre = mm(half, wtok[...])
+            pre = mm(half, wtok[...], NT)
             g1 = jax.nn.sigmoid(pre)
             acts[s, span, :] = (pre * g1).astype(BF)
             spread = mm(member[:, span], tok_grad[s], TN)
             ag = (spread * (g1 * (1.0 + pre * (1.0 - g1)))).astype(BF)
             ags[s, span, :] = ag
-            mt = mm(ag, wtok[...], NT).astype(BF)
+            mt = mm(ag, wtok[...]).astype(BF)
             for g in range(groups):
                 mtc[c * rows + s * Q_WIN : c * rows + (s + 1) * Q_WIN, g * lanes : (g + 1) * lanes] = mt[
                     g * Q_WIN : (g + 1) * Q_WIN, :
@@ -352,7 +360,9 @@
         p_copies[k - 1].wait_recv()
         pair_own = pair_own + precv[k].astype(F32)
     pair_own = exchange_outer(pair_own, 2)
-    gpair_out[...] = pair_own[:, 0:1] * factor
+    across = iota((channels, lanes), 0) == iota((channels, lanes), 1)
+    pair_row = jnp.sum(jnp.where(across, pair_own, 0.0), axis=0, keepdims=True)
+    gpair_out[...] = pair_row[:, :channels] * factor
 
     def arrived(copies, res):
         for k in range(1, inner):
@@ -360,11 +370,11 @@
         return jnp.concatenate([res[j] for j in range(inner)], axis=0).astype(F32) * factor
 
     whole = arrived(eg_copies, eres)
-    gtok_out[...] = whole[0:token_cols].T
+    gtok_out[...] = whole[0:token_cols]
     gout_out[...] = whole[token_cols : token_cols + depth]
     whole = arrived(lg_copies, lres)
     for f in range(4):
-        gproj_out[f] = whole[f * depth : (f + 1) * depth].T
+        gproj_out[f] = whole[f * depth : (f + 1) * depth]
     for copy in sends:
         copy.wait_send()
 
@@ -397,7 +407,14 @@
 
     packed = chunks * rows
     scratch = [
+        vm(samples, atoms, width),
         vm(atoms * channels, K_WIN),
+        vm(1, atoms, dtype=jnp.int32),
+        vm(4, depth, width),
+        vm(depth, width),
+        vm(1, channels),
+        vm(token_cols, width),
+        vm(samples, slots, token_cols),
         vm(2, samples, RIM, width),
         vm(samples, atoms + 2 * RIM, width),
         vm(heads, depth, width),
@@ -435,7 +452,7 @@
         vm(inner, channels, lanes),
         vm(inner, l_piece, lanes),
         vm(3, outer, max(e_piece, l_piece, channels), lanes),
-        pltpu.SemaphoreType.DMA,
+        pltpu.SemaphoreType.DMA((8,)),
         sems(2),
         sems(heads - 1),
         sems(heads - 1, chunks),
@@ -449,31 +466,50 @@
         sems(3, far),
     ]
     in_vmem = pl.BlockSpec(memory_space=pltpu.VMEM)
-    return pl.pallas_call(
+    in_hbm = pl.BlockSpec(memory_space=pltpu.HBM)
+    shapes = (
+        jax.ShapeDtypeStruct((samples, slots, token_cols), BF),
+        jax.ShapeDtypeStruct((4, depth, width), F32),
+        jax.ShapeDtypeStruct((depth, width), F32),
+        jax.ShapeDtypeStruct((1, channels), F32),
+        jax.ShapeDtypeStruct((token_cols, width), F32),
+    )
+    results = pl.pallas_call(
         functools.partial(kernel, n, heads, inner),
-        out_shape=(
-            jax.ShapeDtypeStruct((samples, slots, token_cols), BF),
-            jax.ShapeDtypeStruct((4, width, depth), F32),
-            jax.ShapeDtypeStruct((depth, width), F32),
-            jax.ShapeDtypeStruct((channels, 1), F32),
-            jax.ShapeDtypeStruct((width, token_cols), F32),
-        ),
-        in_specs=[in_vmem, pl.BlockSpec(memory_space=pl.ANY)] + [in_vmem] * 6,
+        out_shape=shapes,
+        in_specs=[in_hbm] * 8,
         out_specs=[in_vmem] * 5,
         scratch_shapes=scratch,
         compiler_params=pltpu.CompilerParams(
-            collective_id=0, has_side_effects=True, vmem_limit_bytes=48 * 1024 * 1024
+            collective_id=0, has_side_effects=True, vmem_limit_bytes=67043328
         ),
     )(
         atom_feats,
         pair_feats.reshape(atoms * channels, K_WIN),
         tok_slot.reshape(1, atoms),
-        w_proj,
+        jnp.swapaxes(w_proj, 1, 2),
         w_out,
-        w_pair,
-        w_tok,
+        w_pair.T,
+        w_tok.T,
         d_tok,
     )
+    tok_act, grad_proj, grad_out, grad_pair, grad_tok = pl.pallas_call(
+        store,
+        out_shape=shapes,
+        in_specs=[in_vmem] * 5,
+        out_specs=[in_hbm] * 5,
+        scratch_shapes=[pltpu.SemaphoreType.DMA((5,))],
+    )(*results)
+    return tok_act, jnp.swapaxes(grad_proj, 1, 2), grad_out, grad_pair.T, grad_tok.T
+
+
+def store(*refs):
+    sem = refs[10]
+    copies = [pltpu.make_async_copy(refs[i], refs[5 + i], sem.at[i]) for i in range(5)]
+    for copy in copies:
+        copy.start()
+    for copy in copies:
+        copy.wait()
 
 
 def solution(mesh):

time: 55.9 us -> 47 us (0.84)
  local copies, waits for them, and re-layouts: 10.5 us -> 0 us
  Pallas kernels: 44.3 us -> 46.2 us
    unnamed x15 -> x0, local copies, waits for them, and re-layouts: 8.41 us -> none
    pallas_call x3 -> x0, local copies, waits for them, and re-layouts: 2.06 us -> none  [on_device(): pl.pallas_call(functools.partial(kernel, n, heads, inner), out_shape=(jax...]
    pallas_call x1 -> x2, Pallas kernels: 44.3 us -> 46.2 us  [the longest x1 44.5 us: on_device(): pl.pallas_call(functools.partial(kernel, n, heads, inner), out_shape=shap...]
where the time goes in v2:
time: 47 us; the launch traced here: 46.8 us
  Pallas kernels  46.2 us (98%)
  between operations  0.64 us (1%)
    pallas_call x1, Pallas kernels, on_device(): pl.pallas_call(functools.partial(kernel, n, heads, inner), out_shape=shap...  44.5 us
    pallas_call x1, Pallas kernels, on_device(): pl.pallas_call(store, out_shape=shapes, in_specs=[in_vmem] * 5, out_specs...  1.7 us

profile of v2, /device:TPU:0, one launch (start us, length us, event | category | flops | bytes accessed | tf_op | source)
XLA Modules:
  0.0 46.8 jit_solution(9613085491221700641)
XLA Ops:
  0.6 44.5 %shard_map.119 = (bf16[2,32,192]{2,1,0:T(8,128)(2,1)}, f32[4,32,128]{2,1,0:T(8,128)}, f32[32,128]{1,0:T(8,128)}, f32[1,16]{1,0:T(1,128)}, f32[192,128]{1,0:T(8,128)}) custom-call(bf16[2,512,128]{2,1,0:T(8,128)(2,1)} %feats_in.1, bf16[8192,128]{1,0:T(8,128)(2,1)} %bitcast.8, s32[1,512]{1,0:T(1,128)} %bitcast.11, bf16[4,32,128]{2,1,0:T(8,128)(2,1)} %bitcast.10, ...), custom_call_target="tpu_custom_call" | custom-call | tf_op jit(solution)/shard_map/pallas_call | solution.py:477
  45.1 1.7 %shard_map.120 = (bf16[2,32,192]{2,1,0:T(8,128)(2,1)}, f32[4,32,128]{2,1,0:T(8,128)}, f32[32,128]{1,0:T(8,128)}, f32[1,16]{1,0:T(1,128)}, f32[192,128]{1,0:T(8,128)}) custom-call(bf16[2,32,192]{2,1,0:T(8,128)(2,1)} %get-tuple-element.15.refs_0_, f32[4,32,128]{2,1,0:T(8,128)} %get-tuple-element.16.refs_1_, f32[32,128]{1,0:T(8,128)} %get-tuple-element.17.refs_2_, ...), custom_call_target="tpu_custom_call" | custom-call | tf_op jit(solution)/shard_map/pallas_call | solution.py:496

commit v3 on v2

--- a/solution.py
+++ b/solution.py
@@ -113,12 +113,6 @@
         bdv[span, :] = jnp.where(keep, wide[2], 0.0).astype(BF)
     wo[0] = wout[...]
 
-    pl.semaphore_wait(barrier, len(greeted))
-
-    to_left = send(feats.at[:, 0:RIM, :], halo.at[1], halo_sem, (1,), ring_peer(-1))
-    to_right = send(feats.at[:, atoms - RIM : atoms, :], halo.at[0], halo_sem, (0,), ring_peer(1))
-    wo_copies = [send(wout, wo.at[k], wo_sem, (k - 1,), head_peer(k)) for k in range(1, heads)]
-
     for c in range(chunks):
         for s in range(samples):
             for g in range(groups):
@@ -150,20 +144,28 @@
     for b in range(chunks * groups):
         bias[b] = mm(mixer, pair[b * flat : (b + 1) * flat, :])
 
-    for k in range(heads):
-        if k:
-            wo_copies[k - 1].wait_recv()
-        tall = jnp.concatenate([wo[k]] * groups, axis=0).astype(F32)
-        for g in range(groups):
-            wbig[k * lanes : (k + 1) * lanes, g * lanes : (g + 1) * lanes] = jnp.where(
-                row_group == g, tall, 0.0
-            ).astype(BF)
-
-    to_right.wait_recv()
-    to_left.wait_recv()
-    for s in range(samples):
-        nx[s, 0:RIM, :] = layer_norm(halo[0, s])
-        nx[s, RIM + atoms : RIM + atoms + RIM, :] = layer_norm(halo[1, s])
+    pl.semaphore_wait(barrier, len(greeted))
+
+    to_left = send(feats.at[:, 0:RIM, :], halo.at[1], halo_sem, (1,), ring_peer(-1))
+    to_right = send(feats.at[:, atoms - RIM : atoms, :], halo.at[0], halo_sem, (0,), ring_peer(1))
+    wo_copies = [send(wout, wo.at[k], wo_sem, (k - 1,), head_peer(k)) for k in range(1, heads)]
+
+    def output_weights():
+        for k in range(heads):
+            if k:
+                wo_copies[k - 1].wait_recv()
+            tall = jnp.concatenate([wo[k]] * groups, axis=0).astype(F32)
+            for g in range(groups):
+                wbig[k * lanes : (k + 1) * lanes, g * lanes : (g + 1) * lanes] = jnp.where(
+                    row_group == g, tall, 0.0
+                ).astype(BF)
+
+    def halo_rows():
+        to_right.wait_recv()
+        to_left.wait_recv()
+        for s in range(samples):
+            nx[s, 0:RIM, :] = layer_norm(halo[0, s])
+            nx[s, RIM + atoms : RIM + atoms + RIM, :] = layer_norm(halo[1, s])
 
     h_copies, o_copies = {}, {}
 
@@ -256,14 +258,21 @@
             pair_terms[0] = term if pair_terms[0] is None else pair_terms[0] + term
         qgp[at_rows, :] = (scale * mm(ycat[at_rows, :], bdk[...])).astype(BF)
 
+    reach = K_WIN - Q_WIN - RIM
+    edges = [c for c in range(chunks) if c * step < RIM or (c + 1) * step + reach > atoms]
+    turn = [c for c in range(chunks) if c not in edges] + edges
     order = []
     for t in range(chunks + 3):
         if t < chunks:
-            order.append((forward, t))
+            if turn[t] == edges[0]:
+                order.append((lambda c: halo_rows(), 0))
+            order.append((forward, turn[t]))
         if 0 <= t - 1 < chunks:
-            order.append((middle, t - 1))
+            if t == 1:
+                order.append((lambda c: output_weights(), 0))
+            order.append((middle, turn[t - 1]))
         if t - 3 >= 0:
-            order.append((backward, t - 3))
+            order.append((backward, turn[t - 3]))
     late = [entry for entry in order if entry[0] is backward][1:]
     for step_of, c in [entry for entry in order if entry not in late]:
         step_of(c)

time: 47 us -> 43.7 us (0.930)
  Pallas kernels: 46.2 us -> 42.9 us
    pallas_call x1, Pallas kernels: 44.5 us -> 41.2 us  [on_device(): pl.pallas_call(functools.partial(kernel, n, heads, inner), out_shape=shap...]
where the time goes in v3:
time: 43.7 us; the launch traced here: 43.6 us
  Pallas kernels  42.9 us (98%)
  between operations  0.64 us (1%)
    pallas_call x1, Pallas kernels, on_device(): pl.pallas_call(functools.partial(kernel, n, heads, inner), out_shape=shap...  41.2 us
    pallas_call x1, Pallas kernels, on_device(): pl.pallas_call(store, out_shape=shapes, in_specs=[in_vmem] * 5, out_specs...  1.7 us

profile of v3, /device:TPU:0, one launch (start us, length us, event | category | flops | bytes accessed | tf_op | source)
XLA Modules:
  0.0 43.6 jit_solution(11558314115132692335)
XLA Ops:
  0.6 41.2 %shard_map.119 = (bf16[2,32,192]{2,1,0:T(8,128)(2,1)}, f32[4,32,128]{2,1,0:T(8,128)}, f32[32,128]{1,0:T(8,128)}, f32[1,16]{1,0:T(1,128)}, f32[192,128]{1,0:T(8,128)}) custom-call(bf16[2,512,128]{2,1,0:T(8,128)(2,1)} %feats_in.1, bf16[8192,128]{1,0:T(8,128)(2,1)} %bitcast.8, s32[1,512]{1,0:T(1,128)} %bitcast.11, bf16[4,32,128]{2,1,0:T(8,128)(2,1)} %bitcast.10, ...), custom_call_target="tpu_custom_call" | custom-call | tf_op jit(solution)/shard_map/pallas_call | solution.py:486
  41.9 1.7 %shard_map.120 = (bf16[2,32,192]{2,1,0:T(8,128)(2,1)}, f32[4,32,128]{2,1,0:T(8,128)}, f32[32,128]{1,0:T(8,128)}, f32[1,16]{1,0:T(1,128)}, f32[192,128]{1,0:T(8,128)}) custom-call(bf16[2,32,192]{2,1,0:T(8,128)(2,1)} %get-tuple-element.15.refs_0_, f32[4,32,128]{2,1,0:T(8,128)} %get-tuple-element.16.refs_1_, f32[32,128]{1,0:T(8,128)} %get-tuple-element.17.refs_2_, ...), custom_call_target="tpu_custom_call" | custom-call | tf_op jit(solution)/shard_map/pallas_call | solution.py:505
